TPU v7x, 32 devices: a whole 2x2x4 slice. The times are simulated.
32 devices in a mesh: groups: 2 (over y), tiles: 16 (over z, x, core).
Axes of the slice: x: 2, y: 2, z: 4, core: 2. Of those that a mesh axis runs over, the one named last changes fastest.
Arguments:
- raw: bfloat16 [16, 256, 2048], P(None, ('groups', 'tiles')), parts along dimension 1, may hold values from -40 to 40, as said below
- fir: float32 [64], replicated, may hold values from -0.75 to 0.75
- keep: int32 [16, 256], P(None, ('groups', 'tiles')), parts along dimension 1, may hold values 0 or 1
- table: int32 [16, 2], replicated, may hold values from 0 to 0, as said below
Outputs:
- stacks: bfloat16 [32, 128, 128, 256], P(('groups', 'tiles')), parts along dimension 0
There are 2 independent parts, one for each index of `groups`. A program takes and returns all parts, laid end to end along the dimension named above; an argument that names none is the same for every part. Nothing has to cross between parts.
Inputs may be any that keep to these rules, and one draw needn't show every extreme that they name: `table`: each row holds r <= c. `raw`: a common motion of all channels plus independent noise.
All inputs are finite; a program needn't handle non-finite values. No bound on the sum of `keep` on one device may be relied on, other than what follows from the above.
Results may differ from a plain program's by a relative error of at most 0.0053.
Values may be sent and summed in bfloat16 or wider, within the bound.
A program may use at most 128 MiB of HBM per device.

v0:
```python
import jax
import jax.numpy as jnp
from jax import lax
from jax.sharding import PartitionSpec as P

WINDOWS = 16
TILE = 128
SEG = 512
LAGS = 256
TAPS = 64
DEC = 4
RAW = 2048
NBIN = 256


def filter_band(fir):
    period = 2 * RAW + TAPS
    pattern = jnp.concatenate([fir[:1], jnp.zeros((period - TAPS,), jnp.float32), fir[1:][::-1]])
    tiled = jnp.tile(pattern, SEG)[: SEG * (period - DEC)].reshape(SEG, period - DEC)
    return tiled[:, :RAW]


def filter_block(raw, fir):
    band = filter_band(fir)
    return jnp.einsum("wcm,nm->wcn", raw.astype(jnp.float32), band, precision=lax.Precision.HIGHEST)


def dft_tables():
    steps = jnp.arange(SEG, dtype=jnp.int32)
    freqs = jnp.arange(NBIN, dtype=jnp.int32)
    angle = 2.0 * jnp.pi / SEG * jnp.mod(steps[:, None] * freqs[None, :], SEG).astype(jnp.float32)
    return (jnp.cos(angle), jnp.sin(angle))


def whiten(decimated, keep):
    cosine, sine = dft_tables()
    real_part = jnp.einsum("wcn,nf->wcf", decimated, cosine, precision=lax.Precision.HIGHEST)
    imag_part = -jnp.einsum("wcn,nf->wcf", decimated, sine, precision=lax.Precision.HIGHEST)
    power = real_part * real_part + imag_part * imag_part
    level = jnp.mean(power, -1, keepdims=True)
    scale = keep.astype(jnp.float32)[..., None] / jnp.sqrt(0.5 * power + 0.5 * level + 1e-05)
    return jnp.concatenate([real_part * scale, imag_part * scale], -1).astype(jnp.bfloat16)


def cross_tile(rows, cols):
    half = rows.shape[-1] // 2
    row_re, row_im = (rows[..., :half], rows[..., half:])
    col_re, col_im = (cols[..., :half], cols[..., half:])
    cross_re = jnp.einsum("wif,wjf->ijf", row_re, col_re, preferred_element_type=jnp.float32)
    cross_re = cross_re + jnp.einsum(
        "wif,wjf->ijf", row_im, col_im, preferred_element_type=jnp.float32
    )
    cross_im = jnp.einsum("wif,wjf->ijf", row_re, col_im, preferred_element_type=jnp.float32)
    cross_im = cross_im - jnp.einsum(
        "wif,wjf->ijf", row_im, col_re, preferred_element_type=jnp.float32
    )
    return jnp.concatenate([cross_re, cross_im], -1).astype(jnp.bfloat16)


def lag_rows(freqs, imaginary):
    shifts = jnp.arange(LAGS, dtype=jnp.int32) - LAGS // 2
    angle = 2.0 * jnp.pi / SEG * jnp.mod(freqs[:, None] * shifts[None, :], SEG).astype(jnp.float32)
    weight = jnp.where(freqs == 0, 1.0, 2.0).astype(jnp.float32)[:, None] / jnp.sqrt(
        jnp.float32(WINDOWS * NBIN)
    )
    return jnp.where(imaginary[:, None], -weight * jnp.sin(angle), weight * jnp.cos(angle)).astype(
        jnp.bfloat16
    )


def local(raw, fir, keep, table):
    devices = lax.axis_size("tiles")
    filtered = filter_block(raw, fir)
    channel_sum = lax.psum(jnp.sum(filtered, 1), "tiles")
    common = channel_sum[:, None, :] / (raw.shape[1] * devices)
    whitened = whiten(filtered - common, keep)
    entry = table[lax.axis_index("tiles")]
    row_base = entry[0] * TILE
    col_base = entry[1] * TILE
    offsets = jnp.arange(TILE, dtype=jnp.int32)
    piece = lax.all_gather(whitened, "tiles", axis=1, tiled=True)
    places = jnp.arange(piece.shape[1], dtype=jnp.int32)
    pick_rows = (places[None, :] == row_base + offsets[:, None]).astype(jnp.bfloat16)
    pick_cols = (places[None, :] == col_base + offsets[:, None]).astype(jnp.bfloat16)
    add_rows = jnp.einsum("in,wnf->wif", pick_rows, piece, preferred_element_type=jnp.float32)
    add_cols = jnp.einsum("in,wnf->wif", pick_cols, piece, preferred_element_type=jnp.float32)
    rows = add_rows.astype(jnp.bfloat16)
    cols = add_cols.astype(jnp.bfloat16)
    cross = cross_tile(rows, cols).reshape(TILE * TILE, 2 * NBIN)
    freqs = jnp.concatenate([jnp.arange(NBIN, dtype=jnp.int32)] * 2)
    imaginary = jnp.arange(2 * NBIN, dtype=jnp.int32) >= NBIN
    lags = lag_rows(freqs, imaginary)
    stacked = jnp.dot(cross, lags, preferred_element_type=jnp.float32).astype(jnp.bfloat16)
    return stacked.reshape(1, TILE, TILE, LAGS)


def solution(mesh):
    placed = (P(None, ("groups", "tiles"), None), P(), P(None, ("groups", "tiles")), P())
    return jax.shard_map(
        local,
        mesh=mesh,
        in_specs=placed,
        out_specs=P(("groups", "tiles"), None, None, None),
        check_vma=False,
    )
```

profile of v0, /device:TPU:0, one launch (start us, length us, event | category | flops | bytes accessed | tf_op | source)
XLA Modules:
  0.0 251.8 jit_solution(16928799047254272326)
XLA Ops:
  6.5 0.0 copy-start
  6.5 0.0 all-gather.2.cloned.1.call-start
  6.5 0.8 slice.33
  7.3 0.1 rev.3
  7.4 0.7 concatenate.26
  8.2 3.9 %tile.4 = f32[512,4160]{1,0:T(8,128)} broadcast(f32[4160]{0:T(1024)S(1)} %concatenate.26), dimensions={1} | broadcast | bytes 8536320 | tf_op jit(solution)/shard_map/tile | solution.py:19
  12.0 10.0 %tile.10 = f32[2129920]{0:T(1024)} reshape(f32[512,4160]{1,0:T(8,128)} %tile.4) | data formatting | bytes 17039360 | tf_op jit(solution)/shard_map/tile | solution.py:19
  22.0 7.8 %slice.42 = f32[2127872]{0:T(1024)} slice(f32[2129920]{0:T(1024)} %tile.10), slice={[0:2127872]} | slice | bytes 17022976 | tf_op jit(solution)/shard_map/slice | solution.py:19
  29.8 14.4 %reshape.66 = f32[512,4156]{1,0:T(8,128)} reshape(f32[2127872]{0:T(1024)} %slice.42) | data formatting | bytes 17022976 | tf_op jit(solution)/shard_map/reshape | solution.py:19
  44.1 0.0 copy-done
  44.2 0.0 copy-start.2
  44.2 0.0 copy-start.3
  44.2 4.8 %fusion.70 = (f32[16,512]{1,0:T(8,128)S(1)}, f32[16,8,512]{2,0,1:T(8,128)S(1)}) fusion(bf16[16,8,2048]{2,1,0:T(8,128)(2,1)S(1)} %copy-done, f32[512,4156]{1,0:T(8,128)} %reshape.66), kind=kOutput, calls=%fused_computation.98 | convolution fusion | flops 1610670080 | bytes 5013504 | tf_op jit(solution)/shard_map/wcm,nm->wcn/dot_general | solution.py:25
  49.0 62.9 %psum.7 = f32[16,512]{1,0:T(8,128)S(1)} all-reduce(f32[16,512]{1,0:T(8,128)S(1)} %get-tuple-element.15), channel_id=1, replica_groups=mesh['groups'=2,'tiles'=16] {'tiles'}, use_global_device_ids=true, to_apply=%region_1.0 | all-reduce | flops 8192 | bytes 65536 | tf_op jit(solution)/shard_map/psum | solution.py:74
  112.0 2.4 fusion.25
  114.4 2.5 fusion.46
  116.9 0.0 copy-done.2
  116.9 0.1 copy.19
  117.0 0.1 multiply_convert_fusion.1
  117.1 0.7 pad_maximum_fusion
  117.7 0.0 all-gather.2.cloned.1.call-update
  117.8 0.0 copy-done.3
  117.8 0.1 constant_dynamic-slice_fusion
  117.9 0.6 fusion.69
  119.8 36.6 %all-gather.2.cloned.1.call-done = bf16[16,128,512]{2,1,0:T(8,128)(2,1)} async-done(((bf16[16,8,512]{2,1,0:T(8,128)(2,1)}), bf16[16,128,512]{2,1,0:T(8,128)(2,1)}) %all-gather.2.cloned.1.call-update) | async-done | bytes 2097168 | tf_op jit(solution)/shard_map/all_gather | solution.py:81
  156.4 2.4 convert_bitcast_fusion
  158.8 2.4 convert_bitcast_fusion.1
  161.2 0.3 fusion.67
  161.5 8.1 %fusion.13 = f32[256,128,128]{2,1,0:T(8,128)} fusion(bf16[16,128,256]{1,2,0:T(8,128)(2,1)S(1)} %get-tuple-element.19, bf16[16,128,256]{1,2,0:T(8,128)(2,1)S(1)} %get-tuple-element.5), kind=kOutput, calls=%fused_computation.22 | convolution fusion | flops 134217728 | bytes 18874368 | tf_op jit(solution)/shard_map/wif,wjf->ijf/dot_general | solution.py:49
  169.6 8.1 %fusion.9 = f32[256,128,128]{2,1,0:T(8,128)} fusion(bf16[16,128,256]{1,2,0:T(8,128)(2,1)S(1)} %get-tuple-element.6, bf16[16,128,256]{1,2,0:T(8,128)(2,1)S(1)} %get-tuple-element.19), kind=kOutput, calls=%fused_computation.18 | convolution fusion | flops 134217728 | bytes 18874368 | tf_op jit(solution)/shard_map/wif,wjf->ijf/dot_general | solution.py:53
  177.6 12.9 %fusion.3 = bf16[128,128,256]{0,1,2:T(8,128)(2,1)} fusion(f32[256,128,128]{2,1,0:T(8,128)} %fusion.13, bf16[16,128,256]{1,2,0:T(8,128)(2,1)S(1)} %get-tuple-element.20, bf16[16,128,256]{1,2,0:T(8,128)(2,1)S(1)} %get-tuple-element.6), kind=kOutput, calls=%fused_computation.6 | convolution fusion | flops 142606336 | bytes 27262976 | tf_op jit(solution)/shard_map/wif,wjf->ijf/dot_general | solution.py:50
  190.5 13.5 %copy.25 = bf16[128,128,256]{2,1,0:T(8,128)(2,1)} copy(bf16[128,128,256]{0,1,2:T(8,128)(2,1)} %fusion.3) | data formatting | bytes 16777216 | tf_op jit(solution)/shard_map/add | solution.py:50
  204.0 12.9 %fusion.4 = bf16[128,128,256]{0,1,2:T(8,128)(2,1)} fusion(f32[256,128,128]{2,1,0:T(8,128)} %fusion.9, bf16[16,128,256]{1,2,0:T(8,128)(2,1)S(1)} %get-tuple-element.20, bf16[16,128,256]{1,2,0:T(8,128)(2,1)S(1)} %get-tuple-element.5), kind=kOutput, calls=%fused_computation.7 | convolution fusion | flops 142606336 | bytes 27262976 | tf_op jit(solution)/shard_map/wif,wjf->ijf/dot_general | solution.py:54
  216.9 13.5 %copy.30 = bf16[128,128,256]{2,1,0:T(8,128)(2,1)} copy(bf16[128,128,256]{0,1,2:T(8,128)(2,1)} %fusion.4) | data formatting | bytes 16777216 | tf_op jit(solution)/shard_map/sub | solution.py:54
  230.4 0.0 copy-start.1
  230.4 14.5 %convolution_convert_fusion = bf16[16384,256]{1,0:T(8,128)(2,1)} fusion(bf16[16384,256]{1,0:T(8,128)(2,1)} %bitcast.40, bf16[16384,256]{1,0:T(8,128)(2,1)} %bitcast.39, f32[512]{0:T(512)S(1)} %get-tuple-element.12, s32[256]{0:T(256)S(1)} %iota_add_fusion, s32[512]{0:T(512)S(1)} %pad_add_fusion, f32[512]{0:T(512)S(1)} %get-tuple-element.11, ...), kind=kOutput, calls=%fused_computation | convolution fusion | flops 4335075328 | bytes 25173504 | tf_op jit(solution)/shard_map/dot_general | solution.py:93
  245.0 0.0 copy-done.1
  (12 shorter events, 0.1 us)
Async XLA Ops:
  6.5 37.6 %copy-start = (bf16[16,8,2048]{2,1,0:T(8,128)(2,1)S(1)}, bf16[16,8,2048]{2,1,0:T(8,128)(2,1)}, u32[]{:S(2)}) copy-start(bf16[16,8,2048]{2,1,0:T(8,128)(2,1)} %param.4) | copy-start | bytes 1572868
  6.5 149.9 %all-gather.2.cloned.1.call-start = ((), (), s32[]{:S(2)}) async-start(), calls=%async_computation | async-start | bytes 2228224 | tf_op jit(solution)/shard_map/all_gather | solution.py:81
  44.2 72.7 %copy-start.2 = (s32[16,8]{0,1:T(8,128)S(1)}, s32[16,8]{0,1:T(8,128)}, u32[]{:S(2)}) copy-start(s32[16,8]{0,1:T(8,128)} %param.6) | copy-start | bytes 1540
  44.2 73.6 %copy-start.3 = (s32[16,2]{0,1:T(2,128)S(1)}, s32[16,2]{0,1:T(2,128)}, u32[]{:S(2)}) copy-start(s32[16,2]{0,1:T(2,128)} %param.7) | copy-start | bytes 388
  230.4 14.5 %copy-start.1 = (bf16[16,8,2048]{2,1,0:T(8,128)(2,1)S(1)}, bf16[16,8,2048]{2,1,0:T(8,128)(2,1)}, u32[]{:S(2)}) copy-start(bf16[16,8,2048]{2,1,0:T(8,128)(2,1)} %param.4) | copy-start | bytes 1572868
Sparse Core Ops, SparseCore 0:
  117.9 38.4 all-gather.1
where the time goes:
time: 253 us; the launch traced here: 252 us
  matrix products  71 us (28%)
  local copies, waits for them, and re-layouts  65.6 us (26%)
  blocking collectives  62.9 us (25%)
  waiting for transfers between devices  36.6 us (14%)
  between operations  14.8 us (6%)
    psum x1, blocking collectives, local(): channel_sum = lax.psum(jnp.sum(filtered, 1), 'tiles')  62.9 us
    all_gather x1, waiting for transfers between devices, local(): piece = lax.all_gather(whitened, 'tiles', axis=1, tiled=True)  36.6 us
    dot_general x1, matrix products, local(): jnp.dot(cross, lags, preferred_element_type=jnp.float32)  14.5 us
    reshape x1, local copies, waits for them, and re-layouts, filter_band(): jnp.tile(pattern, SEG)[:SEG * (period - DEC)].reshape(SEG, period - DEC)  14.4 us
    another operation x2, local copies, waits for them, and re-layouts, filter_band(): jnp.tile(pattern, SEG)[:SEG * (period - DEC)].reshape(SEG, period - DEC)  13.8 us
    sub x1, local copies, waits for them, and re-layouts, cross_tile(): cross_im - jnp.einsum('wif,wjf->ijf', row_im, col_re, preferred_element_t...  13.5 us
    add x1, local copies, waits for them, and re-layouts, cross_tile(): cross_re + jnp.einsum('wif,wjf->ijf', row_im, col_im, preferred_element_t...  13.5 us
    dot_general x1, matrix products, cross_tile(): jnp.einsum('wif,wjf->ijf', row_im, col_re, preferred_element_type=jnp.flo...  12.9 us
  transfers between devices with their start and end apart: 1, of which 1 were waited for; matrix products, arithmetic and copies ran while one was open for 0% of the time, Pallas kernels for 0%

commit v1 on v0

--- a/solution.py
+++ b/solution.py
@@ -11,6 +11,16 @@
 DEC = 4
 RAW = 2048
 NBIN = 256
+
+
+def turned_line(block, axis, d):
+    devices = lax.axis_size(axis)
+    held, tiles = (block, [block])
+    for _ in range(devices - 1):
+        held = lax.ppermute(held, axis, [(i, (i + 1) % devices) for i in range(devices)])
+        tiles.insert(0, held)
+    line = jnp.concatenate(tiles, axis=d)
+    return jnp.roll(line, (lax.axis_index(axis) + 1) * block.shape[d], axis=d)
 
 
 def filter_band(fir):
@@ -78,7 +88,7 @@
     row_base = entry[0] * TILE
     col_base = entry[1] * TILE
     offsets = jnp.arange(TILE, dtype=jnp.int32)
-    piece = lax.all_gather(whitened, "tiles", axis=1, tiled=True)
+    piece = turned_line(whitened, "tiles", 1)
     places = jnp.arange(piece.shape[1], dtype=jnp.int32)
     pick_rows = (places[None, :] == row_base + offsets[:, None]).astype(jnp.bfloat16)
     pick_cols = (places[None, :] == col_base + offsets[:, None]).astype(jnp.bfloat16)

time: 253 us -> 304 us (1.20)
  waiting for transfers between devices: 36.6 us -> 104 us
  between operations: 14.8 us -> 1.7 us
  matrix products: 71 us -> 67.9 us
    ppermute x0 -> x15, waiting for transfers between devices: none -> 104 us  [turned_line(): lax.ppermute(held, axis, [(i, (i + 1) % devices) for i in range(devices)])]
    all_gather x1 -> x0, waiting for transfers between devices: 36.6 us -> none  [local(): piece = lax.all_gather(whitened, 'tiles', axis=1, tiled=True)]
  transfers between devices with their start and end apart: 1 -> 15, of which waited for: 1 -> 15; matrix products, arithmetic and copies ran while one was open for 0% -> 0% of each run, Pallas kernels for 0% -> 0%
where the time goes in v1:
time: 304 us; the launch traced here: 303 us
  waiting for transfers between devices  104 us (34%)
  matrix products  67.9 us (22%)
  local copies, waits for them, and re-layouts  65.9 us (22%)
  blocking collectives  62.9 us (21%)
    ppermute x15, waiting for transfers between devices, turned_line(): lax.ppermute(held, axis, [(i, (i + 1) % devices) for i in range(devices)])  104 us
    psum x1, blocking collectives, local(): channel_sum = lax.psum(jnp.sum(filtered, 1), 'tiles')  62.9 us
    dot_general x1, matrix products, local(): jnp.dot(cross, lags, preferred_element_type=jnp.float32)  14.5 us
    reshape x1, local copies, waits for them, and re-layouts, filter_band(): jnp.tile(pattern, SEG)[:SEG * (period - DEC)].reshape(SEG, period - DEC)  14.4 us
    another operation x2, local copies, waits for them, and re-layouts, filter_band(): jnp.tile(pattern, SEG)[:SEG * (period - DEC)].reshape(SEG, period - DEC)  13.8 us
    sub x1, local copies, waits for them, and re-layouts, cross_tile(): cross_im - jnp.einsum('wif,wjf->ijf', row_im, col_re, preferred_element_t...  13.5 us
    add x1, local copies, waits for them, and re-layouts, cross_tile(): cross_re + jnp.einsum('wif,wjf->ijf', row_im, col_im, preferred_element_t...  13.5 us
    dot_general x1, matrix products, cross_tile(): jnp.einsum('wif,wjf->ijf', row_im, col_re, preferred_element_type=jnp.flo...  12.9 us
  transfers between devices with their start and end apart: 15, of which 15 were waited for; matrix products, arithmetic and copies ran while one was open for 0% of the time, Pallas kernels for 0%

profile of v1, /device:TPU:0, one launch (start us, length us, event | category | flops | bytes accessed | tf_op | source)
XLA Modules:
  0.0 303.2 jit_solution(15996956427724556452)
XLA Ops:
  0.0 0.8 slice.33
  0.8 0.1 rev.3
  0.9 0.7 concatenate.32
  1.6 3.9 %tile.4 = f32[512,4160]{1,0:T(8,128)} broadcast(f32[4160]{0:T(1024)S(1)} %concatenate.32), dimensions={1} | broadcast | bytes 8536320 | tf_op jit(solution)/shard_map/tile | solution.py:29
  5.5 9.9 %tile.10 = f32[2129920]{0:T(1024)} reshape(f32[512,4160]{1,0:T(8,128)} %tile.4) | data formatting | bytes 17039360 | tf_op jit(solution)/shard_map/tile | solution.py:29
  15.5 7.8 %slice.42 = f32[2127872]{0:T(1024)} slice(f32[2129920]{0:T(1024)} %tile.10), slice={[0:2127872]} | slice | bytes 17022976 | tf_op jit(solution)/shard_map/slice | solution.py:29
  23.3 14.4 %reshape.66 = f32[512,4156]{1,0:T(8,128)} reshape(f32[2127872]{0:T(1024)} %slice.42) | data formatting | bytes 17022976 | tf_op jit(solution)/shard_map/reshape | solution.py:29
  37.7 4.8 %fusion.74 = (f32[16,512]{1,0:T(8,128)S(1)}, f32[16,8,512]{2,0,1:T(8,128)S(1)}) fusion(bf16[16,8,2048]{2,1,0:T(8,128)(2,1)S(1)} %copy-done, f32[512,4156]{1,0:T(8,128)} %reshape.66), kind=kOutput, calls=%fused_computation.134 | convolution fusion | flops 1610670080 | bytes 5013504 | tf_op jit(solution)/shard_map/wcm,nm->wcn/dot_general | solution.py:35
  42.5 0.0 copy-start.3
  42.5 62.9 %psum.7 = f32[16,512]{1,0:T(8,128)S(1)} all-reduce(f32[16,512]{1,0:T(8,128)S(1)} %get-tuple-element.15), channel_id=1, replica_groups=mesh['groups'=2,'tiles'=16] {'tiles'}, use_global_device_ids=true, to_apply=%region_1.0 | all-reduce | flops 8192 | bytes 65536 | tf_op jit(solution)/shard_map/psum | solution.py:84
  105.5 2.4 fusion.27
  107.9 2.5 fusion.48
  110.4 0.1 copy.21
  110.5 0.1 multiply_convert_fusion.1
  110.6 0.2 collective-permute-start
  110.9 7.1 %collective-permute-done = bf16[16,8,512]{2,1,0:T(8,128)(2,1)S(1)} collective-permute-done((bf16[16,8,512]{2,1,0:T(8,128)(2,1)S(1)}, bf16[16,8,512]{2,1,0:T(8,128)(2,1)S(1)}, u32[]{:S(2)}, u32[]{:S(2)}) %collective-permute-start) | collective-permute-done | bytes 131104 | tf_op jit(solution)/shard_map/ppermute | solution.py:20
  117.9 7.1 %collective-permute-done.1 = bf16[16,8,512]{2,1,0:T(8,128)(2,1)S(1)} collective-permute-done((bf16[16,8,512]{2,1,0:T(8,128)(2,1)S(1)}, bf16[16,8,512]{2,1,0:T(8,128)(2,1)S(1)}, u32[]{:S(2)}, u32[]{:S(2)}) %collective-permute-start.1) | collective-permute-done | bytes 131104 | tf_op jit(solution)/shard_map/ppermute | solution.py:20
  125.0 7.1 %collective-permute-done.2 = bf16[16,8,512]{2,1,0:T(8,128)(2,1)S(1)} collective-permute-done((bf16[16,8,512]{2,1,0:T(8,128)(2,1)S(1)}, bf16[16,8,512]{2,1,0:T(8,128)(2,1)S(1)}, u32[]{:S(2)}, u32[]{:S(2)}) %collective-permute-start.2) | collective-permute-done | bytes 131104 | tf_op jit(solution)/shard_map/ppermute | solution.py:20
  132.1 0.0 collective-permute-start.3
  132.1 7.1 %collective-permute-done.3 = bf16[16,8,512]{2,1,0:T(8,128)(2,1)S(1)} collective-permute-done((bf16[16,8,512]{2,1,0:T(8,128)(2,1)S(1)}, bf16[16,8,512]{2,1,0:T(8,128)(2,1)S(1)}, u32[]{:S(2)}, u32[]{:S(2)}) %collective-permute-start.3) | collective-permute-done | bytes 131104 | tf_op jit(solution)/shard_map/ppermute | solution.py:20
  139.2 0.0 collective-permute-start.4
  139.2 7.1 %collective-permute-done.4 = bf16[16,8,512]{2,1,0:T(8,128)(2,1)S(1)} collective-permute-done((bf16[16,8,512]{2,1,0:T(8,128)(2,1)S(1)}, bf16[16,8,512]{2,1,0:T(8,128)(2,1)S(1)}, u32[]{:S(2)}, u32[]{:S(2)}) %collective-permute-start.4) | collective-permute-done | bytes 131104 | tf_op jit(solution)/shard_map/ppermute | solution.py:20
  146.3 7.1 %collective-permute-done.5 = bf16[16,8,512]{2,1,0:T(8,128)(2,1)S(1)} collective-permute-done((bf16[16,8,512]{2,1,0:T(8,128)(2,1)S(1)}, bf16[16,8,512]{2,1,0:T(8,128)(2,1)S(1)}, u32[]{:S(2)}, u32[]{:S(2)}) %collective-permute-start.5) | collective-permute-done | bytes 131104 | tf_op jit(solution)/shard_map/ppermute | solution.py:20
  153.4 0.0 collective-permute-start.6
  153.4 7.1 %collective-permute-done.6 = bf16[16,8,512]{2,1,0:T(8,128)(2,1)S(1)} collective-permute-done((bf16[16,8,512]{2,1,0:T(8,128)(2,1)S(1)}, bf16[16,8,512]{2,1,0:T(8,128)(2,1)S(1)}, u32[]{:S(2)}, u32[]{:S(2)}) %collective-permute-start.6) | collective-permute-done | bytes 131104 | tf_op jit(solution)/shard_map/ppermute | solution.py:20
  160.5 0.0 collective-permute-start.7
  160.5 7.1 %collective-permute-done.7 = bf16[16,8,512]{2,1,0:T(8,128)(2,1)S(1)} collective-permute-done((bf16[16,8,512]{2,1,0:T(8,128)(2,1)S(1)}, bf16[16,8,512]{2,1,0:T(8,128)(2,1)S(1)}, u32[]{:S(2)}, u32[]{:S(2)}) %collective-permute-start.7) | collective-permute-done | bytes 131104 | tf_op jit(solution)/shard_map/ppermute | solution.py:20
  167.6 7.1 %collective-permute-done.8 = bf16[16,8,512]{2,1,0:T(8,128)(2,1)S(1)} collective-permute-done((bf16[16,8,512]{2,1,0:T(8,128)(2,1)S(1)}, bf16[16,8,512]{2,1,0:T(8,128)(2,1)S(1)}, u32[]{:S(2)}, u32[]{:S(2)}) %collective-permute-start.8) | collective-permute-done | bytes 131104 | tf_op jit(solution)/shard_map/ppermute | solution.py:20
  174.7 0.0 collective-permute-start.9
  174.7 7.1 %collective-permute-done.9 = bf16[16,8,512]{2,1,0:T(8,128)(2,1)S(1)} collective-permute-done((bf16[16,8,512]{2,1,0:T(8,128)(2,1)S(1)}, bf16[16,8,512]{2,1,0:T(8,128)(2,1)S(1)}, u32[]{:S(2)}, u32[]{:S(2)}) %collective-permute-start.9) | collective-permute-done | bytes 131104 | tf_op jit(solution)/shard_map/ppermute | solution.py:20
  181.7 0.0 collective-permute-start.10
  181.8 7.1 %collective-permute-done.10 = bf16[16,8,512]{2,1,0:T(8,128)(2,1)S(1)} collective-permute-done((bf16[16,8,512]{2,1,0:T(8,128)(2,1)S(1)}, bf16[16,8,512]{2,1,0:T(8,128)(2,1)S(1)}, u32[]{:S(2)}, u32[]{:S(2)}) %collective-permute-start.10) | collective-permute-done | bytes 131104 | tf_op jit(solution)/shard_map/ppermute | solution.py:20
  188.8 0.1 constant_dynamic-slice_fusion
  188.9 0.5 fusion.73
  189.5 6.5 %collective-permute-done.11 = bf16[16,8,512]{2,1,0:T(8,128)(2,1)S(1)} collective-permute-done((bf16[16,8,512]{2,1,0:T(8,128)(2,1)S(1)}, bf16[16,8,512]{2,1,0:T(8,128)(2,1)S(1)}, u32[]{:S(2)}, u32[]{:S(2)}) %collective-permute-start.11) | collective-permute-done | bytes 131104 | tf_op jit(solution)/shard_map/ppermute | solution.py:20
  196.6 6.4 %collective-permute-done.12 = bf16[16,8,512]{2,1,0:T(8,128)(2,1)S(1)} collective-permute-done((bf16[16,8,512]{2,1,0:T(8,128)(2,1)S(1)}, bf16[16,8,512]{2,1,0:T(8,128)(2,1)S(1)}, u32[]{:S(2)}, u32[]{:S(2)}) %collective-permute-start.12) | collective-permute-done | bytes 131104 | tf_op jit(solution)/shard_map/ppermute | solution.py:20
  203.7 6.4 %collective-permute-done.13 = bf16[16,8,512]{2,1,0:T(8,128)(2,1)S(1)} collective-permute-done((bf16[16,8,512]{2,1,0:T(8,128)(2,1)S(1)}, bf16[16,8,512]{2,1,0:T(8,128)(2,1)S(1)}, u32[]{:S(2)}, u32[]{:S(2)}) %collective-permute-start.13) | collective-permute-done | bytes 131104 | tf_op jit(solution)/shard_map/ppermute | solution.py:20
  210.1 7.1 %collective-permute-done.14 = bf16[16,8,512]{2,1,0:T(8,128)(2,1)S(1)} collective-permute-done((bf16[16,8,512]{2,1,0:T(8,128)(2,1)S(1)}, bf16[16,8,512]{2,1,0:T(8,128)(2,1)S(1)}, u32[]{:S(2)}, u32[]{:S(2)}) %collective-permute-start.14) | collective-permute-done | bytes 131104 | tf_op jit(solution)/shard_map/ppermute | solution.py:20
  217.8 0.8 convert_bitcast_fusion
  218.6 0.8 convert_bitcast_fusion.1
  219.4 0.3 fusion.71
  219.7 8.1 %fusion.15 = f32[256,128,128]{2,1,0:T(8,128)} fusion(bf16[16,128,256]{1,2,0:T(8,128)(2,1)S(1)} %get-tuple-element.19, bf16[16,128,256]{1,2,0:T(8,128)(2,1)S(1)} %get-tuple-element.5), kind=kOutput, calls=%fused_computation.24 | convolution fusion | flops 134217728 | bytes 18874368 | tf_op jit(solution)/shard_map/wif,wjf->ijf/dot_general | solution.py:59
  227.8 8.1 %fusion.11 = f32[256,128,128]{2,1,0:T(8,128)} fusion(bf16[16,128,256]{1,2,0:T(8,128)(2,1)S(1)} %get-tuple-element.6, bf16[16,128,256]{1,2,0:T(8,128)(2,1)S(1)} %get-tuple-element.19), kind=kOutput, calls=%fused_computation.20 | convolution fusion | flops 134217728 | bytes 18874368 | tf_op jit(solution)/shard_map/wif,wjf->ijf/dot_general | solution.py:63
  235.9 12.9 %fusion.3 = bf16[128,128,256]{0,1,2:T(8,128)(2,1)} fusion(f32[256,128,128]{2,1,0:T(8,128)} %fusion.15, bf16[16,128,256]{1,2,0:T(8,128)(2,1)S(1)} %get-tuple-element.20, bf16[16,128,256]{1,2,0:T(8,128)(2,1)S(1)} %get-tuple-element.6), kind=kOutput, calls=%fused_computation.6 | convolution fusion | flops 142606336 | bytes 27262976 | tf_op jit(solution)/shard_map/wif,wjf->ijf/dot_general | solution.py:60
  248.8 13.5 %copy.29 = bf16[128,128,256]{2,1,0:T(8,128)(2,1)} copy(bf16[128,128,256]{0,1,2:T(8,128)(2,1)} %fusion.3) | data formatting | bytes 16777216 | tf_op jit(solution)/shard_map/add | solution.py:60
  262.3 12.9 %fusion.4 = bf16[128,128,256]{0,1,2:T(8,128)(2,1)} fusion(f32[256,128,128]{2,1,0:T(8,128)} %fusion.11, bf16[16,128,256]{1,2,0:T(8,128)(2,1)S(1)} %get-tuple-element.20, bf16[16,128,256]{1,2,0:T(8,128)(2,1)S(1)} %get-tuple-element.5), kind=kOutput, calls=%fused_computation.7 | convolution fusion | flops 142606336 | bytes 27262976 | tf_op jit(solution)/shard_map/wif,wjf->ijf/dot_general | solution.py:64
  275.2 13.5 %copy.34 = bf16[128,128,256]{2,1,0:T(8,128)(2,1)} copy(bf16[128,128,256]{0,1,2:T(8,128)(2,1)} %fusion.4) | data formatting | bytes 16777216 | tf_op jit(solution)/shard_map/sub | solution.py:64
  288.7 14.5 %convolution_convert_fusion = bf16[16384,256]{1,0:T(8,128)(2,1)} fusion(bf16[16384,256]{1,0:T(8,128)(2,1)} %bitcast.38, bf16[16384,256]{1,0:T(8,128)(2,1)} %bitcast.37, f32[512]{0:T(512)S(1)} %get-tuple-element.12, s32[256]{0:T(256)S(1)} %iota_add_fusion, s32[512]{0:T(512)S(1)} %pad_add_fusion, f32[512]{0:T(512)S(1)} %get-tuple-element.11, ...), kind=kOutput, calls=%fused_computation | convolution fusion | flops 4335075328 | bytes 25173504 | tf_op jit(solution)/shard_map/dot_general | solution.py:103
  (60 shorter events, 0.5 us)
Async XLA Ops:
  0.0 37.7 %copy-start = (bf16[16,8,2048]{2,1,0:T(8,128)(2,1)S(1)}, bf16[16,8,2048]{2,1,0:T(8,128)(2,1)}, u32[]{:S(2)}) copy-start(bf16[16,8,2048]{2,1,0:T(8,128)(2,1)} %param.4) | copy-start | bytes 1572868
  37.7 72.7 %copy-start.2 = (s32[16,8]{0,1:T(8,128)S(1)}, s32[16,8]{0,1:T(8,128)}, u32[]{:S(2)}) copy-start(s32[16,8]{0,1:T(8,128)} %param.6) | copy-start | bytes 1540
  42.5 146.3 %copy-start.3 = (s32[16,2]{0,1:T(2,128)S(1)}, s32[16,2]{0,1:T(2,128)}, u32[]{:S(2)}) copy-start(s32[16,2]{0,1:T(2,128)} %param.7) | copy-start | bytes 388
  110.6 7.3 %collective-permute-start = (bf16[16,8,512]{2,1,0:T(8,128)(2,1)S(1)}, bf16[16,8,512]{2,1,0:T(8,128)(2,1)S(1)}, u32[]{:S(2)}, u32[]{:S(2)}) collective-permute-start(bf16[16,8,512]{2,1,0:T(8,128)(2,1)S(1)} %pad_maximum_fusion), channel_id=1, source_target_pairs={{0,1},{1,2},{2,3},{3,4},{4,5},{5,6},{6,7},{7,8},{8,9},{9,10},{10,1... | collective-permute-start | bytes 393224 | tf_op jit(solution)/shard_map/ppermute | solution.py:20
  117.9 7.1 %collective-permute-start.1 = (bf16[16,8,512]{2,1,0:T(8,128)(2,1)S(1)}, bf16[16,8,512]{2,1,0:T(8,128)(2,1)S(1)}, u32[]{:S(2)}, u32[]{:S(2)}) collective-permute-start(bf16[16,8,512]{2,1,0:T(8,128)(2,1)S(1)} %collective-permute-done), channel_id=1, source_target_pairs={{0,1},{1,2},{2,3},{3,4},{4,5},{5,6},{6,7},{7,8},{8,9},{9,10},{10,1... | collective-permute-start | bytes 393224 | tf_op jit(solution)/shard_map/ppermute | solution.py:20
  125.0 7.1 %collective-permute-start.2 = (bf16[16,8,512]{2,1,0:T(8,128)(2,1)S(1)}, bf16[16,8,512]{2,1,0:T(8,128)(2,1)S(1)}, u32[]{:S(2)}, u32[]{:S(2)}) collective-permute-start(bf16[16,8,512]{2,1,0:T(8,128)(2,1)S(1)} %collective-permute-done.1), channel_id=1, source_target_pairs={{0,1},{1,2},{2,3},{3,4},{4,5},{5,6},{6,7},{7,8},{8,9},{9,10},{10,1... | collective-permute-start | bytes 393224 | tf_op jit(solution)/shard_map/ppermute | solution.py:20
  132.1 7.1 %collective-permute-start.3 = (bf16[16,8,512]{2,1,0:T(8,128)(2,1)S(1)}, bf16[16,8,512]{2,1,0:T(8,128)(2,1)S(1)}, u32[]{:S(2)}, u32[]{:S(2)}) collective-permute-start(bf16[16,8,512]{2,1,0:T(8,128)(2,1)S(1)} %collective-permute-done.2), channel_id=1, source_target_pairs={{0,1},{1,2},{2,3},{3,4},{4,5},{5,6},{6,7},{7,8},{8,9},{9,10},{10,1... | collective-permute-start | bytes 393224 | tf_op jit(solution)/shard_map/ppermute | solution.py:20
  139.2 7.1 %collective-permute-start.4 = (bf16[16,8,512]{2,1,0:T(8,128)(2,1)S(1)}, bf16[16,8,512]{2,1,0:T(8,128)(2,1)S(1)}, u32[]{:S(2)}, u32[]{:S(2)}) collective-permute-start(bf16[16,8,512]{2,1,0:T(8,128)(2,1)S(1)} %collective-permute-done.3), channel_id=1, source_target_pairs={{0,1},{1,2},{2,3},{3,4},{4,5},{5,6},{6,7},{7,8},{8,9},{9,10},{10,1... | collective-permute-start | bytes 393224 | tf_op jit(solution)/shard_map/ppermute | solution.py:20
  146.3 7.1 %collective-permute-start.5 = (bf16[16,8,512]{2,1,0:T(8,128)(2,1)S(1)}, bf16[16,8,512]{2,1,0:T(8,128)(2,1)S(1)}, u32[]{:S(2)}, u32[]{:S(2)}) collective-permute-start(bf16[16,8,512]{2,1,0:T(8,128)(2,1)S(1)} %collective-permute-done.4), channel_id=1, source_target_pairs={{0,1},{1,2},{2,3},{3,4},{4,5},{5,6},{6,7},{7,8},{8,9},{9,10},{10,1... | collective-permute-start | bytes 393224 | tf_op jit(solution)/shard_map/ppermute | solution.py:20
  153.4 7.1 %collective-permute-start.6 = (bf16[16,8,512]{2,1,0:T(8,128)(2,1)S(1)}, bf16[16,8,512]{2,1,0:T(8,128)(2,1)S(1)}, u32[]{:S(2)}, u32[]{:S(2)}) collective-permute-start(bf16[16,8,512]{2,1,0:T(8,128)(2,1)S(1)} %collective-permute-done.5), channel_id=1, source_target_pairs={{0,1},{1,2},{2,3},{3,4},{4,5},{5,6},{6,7},{7,8},{8,9},{9,10},{10,1... | collective-permute-start | bytes 393224 | tf_op jit(solution)/shard_map/ppermute | solution.py:20
  160.5 7.1 %collective-permute-start.7 = (bf16[16,8,512]{2,1,0:T(8,128)(2,1)S(1)}, bf16[16,8,512]{2,1,0:T(8,128)(2,1)S(1)}, u32[]{:S(2)}, u32[]{:S(2)}) collective-permute-start(bf16[16,8,512]{2,1,0:T(8,128)(2,1)S(1)} %collective-permute-done.6), channel_id=1, source_target_pairs={{0,1},{1,2},{2,3},{3,4},{4,5},{5,6},{6,7},{7,8},{8,9},{9,10},{10,1... | collective-permute-start | bytes 393224 | tf_op jit(solution)/shard_map/ppermute | solution.py:20
  167.6 7.1 %collective-permute-start.8 = (bf16[16,8,512]{2,1,0:T(8,128)(2,1)S(1)}, bf16[16,8,512]{2,1,0:T(8,128)(2,1)S(1)}, u32[]{:S(2)}, u32[]{:S(2)}) collective-permute-start(bf16[16,8,512]{2,1,0:T(8,128)(2,1)S(1)} %collective-permute-done.7), channel_id=1, source_target_pairs={{0,1},{1,2},{2,3},{3,4},{4,5},{5,6},{6,7},{7,8},{8,9},{9,10},{10,1... | collective-permute-start | bytes 393224 | tf_op jit(solution)/shard_map/ppermute | solution.py:20
  174.7 7.1 %collective-permute-start.9 = (bf16[16,8,512]{2,1,0:T(8,128)(2,1)S(1)}, bf16[16,8,512]{2,1,0:T(8,128)(2,1)S(1)}, u32[]{:S(2)}, u32[]{:S(2)}) collective-permute-start(bf16[16,8,512]{2,1,0:T(8,128)(2,1)S(1)} %collective-permute-done.8), channel_id=1, source_target_pairs={{0,1},{1,2},{2,3},{3,4},{4,5},{5,6},{6,7},{7,8},{8,9},{9,10},{10,1... | collective-permute-start | bytes 393224 | tf_op jit(solution)/shard_map/ppermute | solution.py:20
  181.7 7.1 %collective-permute-start.10 = (bf16[16,8,512]{2,1,0:T(8,128)(2,1)S(1)}, bf16[16,8,512]{2,1,0:T(8,128)(2,1)S(1)}, u32[]{:S(2)}, u32[]{:S(2)}) collective-permute-start(bf16[16,8,512]{2,1,0:T(8,128)(2,1)S(1)} %collective-permute-done.9), channel_id=1, source_target_pairs={{0,1},{1,2},{2,3},{3,4},{4,5},{5,6},{6,7},{7,8},{8,9},{9,10},{10,1... | collective-permute-start | bytes 393224 | tf_op jit(solution)/shard_map/ppermute | solution.py:20
  188.8 7.1 %collective-permute-start.11 = (bf16[16,8,512]{2,1,0:T(8,128)(2,1)S(1)}, bf16[16,8,512]{2,1,0:T(8,128)(2,1)S(1)}, u32[]{:S(2)}, u32[]{:S(2)}) collective-permute-start(bf16[16,8,512]{2,1,0:T(8,128)(2,1)S(1)} %collective-permute-done.10), channel_id=1, source_target_pairs={{0,1},{1,2},{2,3},{3,4},{4,5},{5,6},{6,7},{7,8},{8,9},{9,10},{10,1... | collective-permute-start | bytes 393224 | tf_op jit(solution)/shard_map/ppermute | solution.py:20
  195.9 7.1 %collective-permute-start.12 = (bf16[16,8,512]{2,1,0:T(8,128)(2,1)S(1)}, bf16[16,8,512]{2,1,0:T(8,128)(2,1)S(1)}, u32[]{:S(2)}, u32[]{:S(2)}) collective-permute-start(bf16[16,8,512]{2,1,0:T(8,128)(2,1)S(1)} %collective-permute-done.11), channel_id=1, source_target_pairs={{0,1},{1,2},{2,3},{3,4},{4,5},{5,6},{6,7},{7,8},{8,9},{9,10},{10,1... | collective-permute-start | bytes 393224 | tf_op jit(solution)/shard_map/ppermute | solution.py:20
  203.0 7.1 %collective-permute-start.13 = (bf16[16,8,512]{2,1,0:T(8,128)(2,1)S(1)}, bf16[16,8,512]{2,1,0:T(8,128)(2,1)S(1)}, u32[]{:S(2)}, u32[]{:S(2)}) collective-permute-start(bf16[16,8,512]{2,1,0:T(8,128)(2,1)S(1)} %collective-permute-done.12), channel_id=1, source_target_pairs={{0,1},{1,2},{2,3},{3,4},{4,5},{5,6},{6,7},{7,8},{8,9},{9,10},{10,1... | collective-permute-start | bytes 393224 | tf_op jit(solution)/shard_map/ppermute | solution.py:20
  210.1 7.1 %collective-permute-start.14 = (bf16[16,8,512]{2,1,0:T(8,128)(2,1)S(1)}, bf16[16,8,512]{2,1,0:T(8,128)(2,1)S(1)}, u32[]{:S(2)}, u32[]{:S(2)}) collective-permute-start(bf16[16,8,512]{2,1,0:T(8,128)(2,1)S(1)} %collective-permute-done.13), channel_id=1, source_target_pairs={{0,1},{1,2},{2,3},{3,4},{4,5},{5,6},{6,7},{7,8},{8,9},{9,10},{10,1... | collective-permute-start | bytes 393224 | tf_op jit(solution)/shard_map/ppermute | solution.py:20
  288.7 14.5 %copy-start.1 = (bf16[16,8,2048]{2,1,0:T(8,128)(2,1)S(1)}, bf16[16,8,2048]{2,1,0:T(8,128)(2,1)}, u32[]{:S(2)}) copy-start(bf16[16,8,2048]{2,1,0:T(8,128)(2,1)} %param.4) | copy-start | bytes 1572868
